TPU v7x, 32 devices: a whole 2x2x4 slice. The times are simulated.
32 devices in a mesh: dp: 16 (over z, y, x), mp: 2 (over core).
Axes of the slice: x: 2, y: 2, z: 4, core: 2. Of those that a mesh axis runs over, the one named last changes fastest.
Arguments:
- tokens: bfloat16 [32, 512, 768], P('dp', 'mp'), may hold values from -6 to 6
- lengths: int32 [32, 16], P('dp'), may hold values from 0 to 512, as said below
- cotangent: bfloat16 [32, 512, 768], P('dp', 'mp'), may hold values from -6 to 6
- w_query: bfloat16 [2, 768, 768], P(None, None, 'mp'), may hold values from -0.21875 to 0.21875
- b_query: bfloat16 [2, 768], P(None, 'mp'), may hold values from -3 to 3
- w_key: bfloat16 [2, 768, 768], P(None, None, 'mp'), may hold values from -0.21875 to 0.21875
- w_value: bfloat16 [2, 768, 768], P(None, None, 'mp'), may hold values from -0.21875 to 0.21875
- b_value: bfloat16 [2, 768], P(None, 'mp'), may hold values from -3 to 3
- w_out: bfloat16 [2, 768, 768], P(None, None, 'mp'), may hold values from -1.75 to 1.75
- b_out: bfloat16 [2, 768], replicated, may hold values from -3 to 3
- first_gain: bfloat16 [2, 768], replicated, may hold values from 0.099609375 to 1.8984375
- first_shift: bfloat16 [2, 768], replicated, may hold values from -3 to 3
- w_up: bfloat16 [2, 768, 3072], P(None, None, 'mp'), may hold values from -0.21875 to 0.21875
- b_up: bfloat16 [2, 3072], P(None, 'mp'), may hold values from -3 to 3
- w_down: bfloat16 [2, 768, 3072], P(None, None, 'mp'), may hold values from -0.109375 to 0.109375
- b_down: bfloat16 [2, 768], replicated, may hold values from -3 to 3
- second_gain: bfloat16 [2, 768], replicated, may hold values from 0.099609375 to 1.8984375
- second_shift: bfloat16 [2, 768], replicated, may hold values from -3 to 3
Outputs:
- encoded: bfloat16 [32, 512, 768], P('dp', 'mp')
- token_grad: float32 [32, 512, 768], P('dp', 'mp')
- grad_w_query: float32 [2, 768, 768], P(None, 'dp', 'mp')
- grad_b_query: float32 [2, 768], P(None, 'mp')
- grad_w_key: float32 [2, 768, 768], P(None, 'dp', 'mp')
- grad_w_value: float32 [2, 768, 768], P(None, 'dp', 'mp')
- grad_b_value: float32 [2, 768], P(None, 'mp')
- grad_w_out: float32 [2, 768, 768], P(None, 'dp', 'mp')
- grad_b_out: float32 [2, 768], replicated
- grad_first_gain: float32 [2, 768], replicated
- grad_first_shift: float32 [2, 768], replicated
- grad_w_up: float32 [2, 768, 3072], P(None, 'dp', 'mp')
- grad_b_up: float32 [2, 3072], P(None, 'mp')
- grad_w_down: float32 [2, 768, 3072], P(None, 'dp', 'mp')
- grad_b_down: float32 [2, 768], replicated
- grad_second_gain: float32 [2, 768], replicated
- grad_second_shift: float32 [2, 768], replicated
Inputs may be any that keep to these rules, and one draw needn't show every extreme that they name: In each row either entries 1 to 15 are 0 and entry 0 is a passage's length, at least 64, or all 16 entries are lengths of queries, each at least 1 and at most 32. Some row holds a passage of 512 slots and some query fills its 32 slots.
All inputs are finite; a program needn't handle non-finite values.
Results may differ from a plain program's by a relative error of at most 0.04.
Values may be sent and summed in bfloat16 or wider, within the bound.
No kernel may reach another device: no remote copies, remote signals or barrier semaphores. Data moves between devices by JAX's collectives and lax.ppermute only.
A program may use at most 192 MiB of HBM per device.

v0:
```python
import jax
import jax.numpy as jnp
from jax import lax
from jax.sharding import PartitionSpec as P

DH = 64
SLOTS = 512
QSLOT = 32
SEGS = 16


def visible_mask(lengths):
    slot_index = jnp.arange(SLOTS, dtype=jnp.int32)
    is_query = lengths[:, 1] > 0
    segment_width = jnp.where(is_query, QSLOT, SLOTS).astype(jnp.int32)[:, None]
    segment = slot_index[None, :] // segment_width
    inside = slot_index[None, :] - segment * segment_width
    onehot = segment[:, :, None] == jnp.arange(SEGS, dtype=jnp.int32)[None, None, :]
    segment_length = jnp.sum(jnp.where(onehot, lengths[:, None, :], 0), axis=2)
    live_keys = inside < segment_length
    same_segment = segment[:, :, None] == segment[:, None, :]
    return same_segment & live_keys[:, None, :]


def layer_norm(residual, norm_gain, norm_shift):
    average = jnp.mean(residual, axis=-1, keepdims=True)
    centred = residual - average
    variance = jnp.mean(centred * centred, axis=-1, keepdims=True)
    return centred * lax.rsqrt(variance + 1e-12) * norm_gain + norm_shift


def gelu_exact(argument):
    return 0.5 * argument * (1.0 + jax.scipy.special.erf(argument * 0.7071067811865476))


def project(left, right):
    return jnp.einsum("rsd,de->rse", left, right, preferred_element_type=jnp.float32)


def attend(row_data):
    row_queries, row_keys, row_values, visible = row_data
    head_count = row_queries.shape[1] // DH
    query_heads = row_queries.reshape(SLOTS, head_count, DH)
    key_heads = row_keys.reshape(SLOTS, head_count, DH)
    value_heads = row_values.reshape(SLOTS, head_count, DH)
    scores = jnp.einsum(
        "shd,thd->hst", query_heads, key_heads, preferred_element_type=jnp.float32
    ) * DH ** (-0.5)
    scores = jnp.where(visible[None], scores, -1000000000.0)
    row_peak = jnp.max(scores, axis=2, keepdims=True)
    exponent = jnp.exp(scores - row_peak)
    summed = jnp.sum(exponent, axis=2, keepdims=True)
    weights_low = (exponent / summed).astype(jnp.bfloat16)
    context = jnp.einsum(
        "hst,thd->shd", weights_low, value_heads, preferred_element_type=jnp.float32
    )
    return (
        context.reshape(SLOTS, head_count * DH).astype(jnp.bfloat16),
        (row_peak + jnp.log(summed))[:, :, 0],
    )


def attend_back(row_data):
    row_queries, row_keys, row_values, visible, log_total, context_grad = row_data
    head_count = row_queries.shape[1] // DH
    width = head_count * DH
    query_heads = row_queries.reshape(SLOTS, head_count, DH)
    key_heads = row_keys.reshape(SLOTS, head_count, DH)
    value_heads = row_values.reshape(SLOTS, head_count, DH)
    grad_heads = context_grad.reshape(SLOTS, head_count, DH)
    scores = jnp.einsum(
        "shd,thd->hst", query_heads, key_heads, preferred_element_type=jnp.float32
    ) * DH ** (-0.5)
    probabilities = jnp.where(visible[None], jnp.exp(scores - log_total[:, :, None]), 0.0)
    weights_low = probabilities.astype(jnp.bfloat16)
    value_grad = jnp.einsum(
        "hst,shd->thd", weights_low, grad_heads, preferred_element_type=jnp.float32
    )
    weight_grad = jnp.einsum(
        "shd,thd->hst", grad_heads, value_heads, preferred_element_type=jnp.float32
    )
    score_grad = (
        probabilities * (weight_grad - jnp.sum(probabilities * weight_grad, axis=2, keepdims=True))
    ).astype(jnp.bfloat16)
    query_grad = jnp.einsum(
        "hst,thd->shd", score_grad, key_heads, preferred_element_type=jnp.float32
    ) * DH ** (-0.5)
    key_grad = jnp.einsum(
        "hst,shd->thd", score_grad, query_heads, preferred_element_type=jnp.float32
    ) * DH ** (-0.5)
    return (
        query_grad.reshape(SLOTS, width).astype(jnp.bfloat16),
        key_grad.reshape(SLOTS, width).astype(jnp.bfloat16),
        value_grad.reshape(SLOTS, width).astype(jnp.bfloat16),
    )


def forward_layer(block_in, weights, visibility):
    (
        w_query,
        b_query,
        w_key,
        w_value,
        b_value,
        w_out,
        b_out,
        first_gain,
        first_shift,
        w_up,
        b_up,
        w_down,
        b_down,
        second_gain,
        second_shift,
    ) = weights
    gathered = lax.all_gather(block_in, "mp", axis=1, tiled=True)
    queries = (project(gathered, w_query) + b_query.astype(jnp.float32)).astype(jnp.bfloat16)
    keys_all = project(gathered, w_key).astype(jnp.bfloat16)
    values_all = (project(gathered, w_value) + b_value.astype(jnp.float32)).astype(jnp.bfloat16)
    context, log_total = lax.map(attend, (queries, keys_all, values_all, visibility))
    partial_out = jnp.einsum("rsc,dc->rsd", context, w_out, preferred_element_type=jnp.float32)
    attended = lax.psum_scatter(
        partial_out.astype(jnp.bfloat16), "mp", scatter_dimension=1, tiled=True
    ).astype(jnp.float32) + b_out.astype(jnp.float32)
    first_resid = block_in.astype(jnp.float32) + attended
    normed = layer_norm(
        first_resid, first_gain.astype(jnp.float32), first_shift.astype(jnp.float32)
    )
    gathered_normed = lax.all_gather(normed.astype(jnp.bfloat16), "mp", axis=1, tiled=True)
    upward = project(gathered_normed, w_up) + b_up.astype(jnp.float32)
    activated = gelu_exact(upward).astype(jnp.bfloat16)
    partial_down = jnp.einsum("rsf,df->rsd", activated, w_down, preferred_element_type=jnp.float32)
    downward = lax.psum_scatter(
        partial_down.astype(jnp.bfloat16), "mp", scatter_dimension=1, tiled=True
    ).astype(jnp.float32) + b_down.astype(jnp.float32)
    second_resid = normed + downward
    output = layer_norm(
        second_resid, second_gain.astype(jnp.float32), second_shift.astype(jnp.float32)
    )
    kept_state = (
        gathered,
        queries,
        keys_all,
        values_all,
        context,
        log_total,
        first_resid,
        gathered_normed,
        upward,
        activated,
        second_resid,
    )
    return (output, kept_state)


def backward_layer(weights, visibility, kept_state, grad_out):
    (
        w_query,
        b_query,
        w_key,
        w_value,
        b_value,
        w_out,
        b_out,
        first_gain,
        first_shift,
        w_up,
        b_up,
        w_down,
        b_down,
        second_gain,
        second_shift,
    ) = weights
    (
        gathered,
        queries,
        keys_all,
        values_all,
        context,
        log_total,
        first_resid,
        gathered_normed,
        upward,
        activated,
        second_resid,
    ) = kept_state
    unused, pull_second = jax.vjp(
        layer_norm, second_resid, second_gain.astype(jnp.float32), second_shift.astype(jnp.float32)
    )
    grad_second, grad_second_gain, grad_second_shift = pull_second(grad_out)
    down_grad = grad_second.astype(jnp.bfloat16)
    grad_b_down = jnp.sum(down_grad, axis=(0, 1), dtype=jnp.float32)
    gathered_down = lax.all_gather(down_grad, "mp", axis=1, tiled=True)
    grad_w_down = jnp.einsum(
        "rsd,rsf->df", gathered_down, activated, preferred_element_type=jnp.float32
    )
    act_grad = jnp.einsum("rsd,df->rsf", gathered_down, w_down, preferred_element_type=jnp.float32)
    unused, pull_gelu = jax.vjp(gelu_exact, upward)
    up_grad = pull_gelu(act_grad)[0].astype(jnp.bfloat16)
    grad_b_up = jnp.sum(up_grad, axis=(0, 1), dtype=jnp.float32)
    grad_w_up = jnp.einsum(
        "rsd,rsf->df", gathered_normed, up_grad, preferred_element_type=jnp.float32
    )
    partial_normed = jnp.einsum("rsf,df->rsd", up_grad, w_up, preferred_element_type=jnp.float32)
    normed_grad = grad_second + lax.psum_scatter(
        partial_normed.astype(jnp.bfloat16), "mp", scatter_dimension=1, tiled=True
    ).astype(jnp.float32)
    unused, pull_first = jax.vjp(
        layer_norm, first_resid, first_gain.astype(jnp.float32), first_shift.astype(jnp.float32)
    )
    grad_first, grad_first_gain, grad_first_shift = pull_first(normed_grad)
    out_grad = grad_first.astype(jnp.bfloat16)
    grad_b_out = jnp.sum(out_grad, axis=(0, 1), dtype=jnp.float32)
    gathered_out = lax.all_gather(out_grad, "mp", axis=1, tiled=True)
    grad_w_out = jnp.einsum(
        "rsd,rsc->dc", gathered_out, context, preferred_element_type=jnp.float32
    )
    context_grad = jnp.einsum(
        "rsd,dc->rsc", gathered_out, w_out, preferred_element_type=jnp.float32
    ).astype(jnp.bfloat16)
    query_grad, key_grad, value_grad = lax.map(
        attend_back, (queries, keys_all, values_all, visibility, log_total, context_grad)
    )
    grad_b_query = jnp.sum(query_grad, axis=(0, 1), dtype=jnp.float32)
    grad_b_value = jnp.sum(value_grad, axis=(0, 1), dtype=jnp.float32)
    grad_w_query = jnp.einsum(
        "rsd,rse->de", gathered, query_grad, preferred_element_type=jnp.float32
    )
    grad_w_key = jnp.einsum("rsd,rse->de", gathered, key_grad, preferred_element_type=jnp.float32)
    grad_w_value = jnp.einsum(
        "rsd,rse->de", gathered, value_grad, preferred_element_type=jnp.float32
    )
    partial_in = jnp.einsum("rse,de->rsd", query_grad, w_query, preferred_element_type=jnp.float32)
    partial_in = partial_in + jnp.einsum(
        "rse,de->rsd", key_grad, w_key, preferred_element_type=jnp.float32
    )
    partial_in = partial_in + jnp.einsum(
        "rse,de->rsd", value_grad, w_value, preferred_element_type=jnp.float32
    )
    block_grad = grad_first + lax.psum_scatter(
        partial_in.astype(jnp.bfloat16), "mp", scatter_dimension=1, tiled=True
    ).astype(jnp.float32)
    gradients = (
        grad_w_query,
        grad_b_query,
        grad_w_key,
        grad_w_value,
        grad_b_value,
        grad_w_out,
        grad_b_out,
        grad_first_gain,
        grad_first_shift,
        grad_w_up,
        grad_b_up,
        grad_w_down,
        grad_b_down,
        grad_second_gain,
        grad_second_shift,
    )
    return (block_grad, gradients)


def shards(
    tokens,
    lengths,
    cotangent,
    w_query,
    b_query,
    w_key,
    w_value,
    b_value,
    w_out,
    b_out,
    first_gain,
    first_shift,
    w_up,
    b_up,
    w_down,
    b_down,
    second_gain,
    second_shift,
):
    params = (
        w_query,
        b_query,
        w_key,
        w_value,
        b_value,
        w_out,
        b_out,
        first_gain,
        first_shift,
        w_up,
        b_up,
        w_down,
        b_down,
        second_gain,
        second_shift,
    )
    visibility = visible_mask(lengths)
    layer_count = w_query.shape[0]
    block_inputs = []
    kept_states = []
    hidden = tokens
    for layer_index in range(layer_count):
        weights = tuple((member[layer_index] for member in params))
        block_inputs.append(hidden)
        output, kept_state = forward_layer(hidden, weights, visibility)
        kept_states.append(kept_state)
        hidden = output.astype(jnp.bfloat16)
    grad_hidden = cotangent.astype(jnp.float32)
    layer_grads = [None] * layer_count
    for layer_index in reversed(range(layer_count)):
        weights = tuple((member[layer_index] for member in params))
        kept_state = forward_layer(block_inputs[layer_index], weights, visibility)[1]
        grad_hidden, gradients = backward_layer(weights, visibility, kept_state, grad_hidden)
        layer_grads[layer_index] = gradients
    stacked = [
        jnp.stack([layer_grads[layer_index][member_index] for layer_index in range(layer_count)])
        for member_index in range(15)
    ]
    matrices = (
        lax.psum_scatter(stacked[0], "dp", scatter_dimension=1, tiled=True),
        lax.psum_scatter(stacked[2], "dp", scatter_dimension=1, tiled=True),
        lax.psum_scatter(stacked[3], "dp", scatter_dimension=1, tiled=True),
        lax.psum_scatter(stacked[5], "dp", scatter_dimension=1, tiled=True),
        lax.psum_scatter(stacked[9], "dp", scatter_dimension=1, tiled=True),
        lax.psum_scatter(stacked[11], "dp", scatter_dimension=1, tiled=True),
    )
    columns = lax.psum((stacked[1], stacked[4], stacked[10]), "dp")
    rows_summed = lax.psum(
        (stacked[6], stacked[7], stacked[8], stacked[12], stacked[13], stacked[14]), ("dp", "mp")
    )
    return (
        hidden,
        grad_hidden,
        matrices[0],
        columns[0],
        matrices[1],
        matrices[2],
        columns[1],
        matrices[3],
        rows_summed[0],
        rows_summed[1],
        rows_summed[2],
        matrices[4],
        columns[2],
        matrices[5],
        rows_summed[3],
        rows_summed[4],
        rows_summed[5],
    )


def solution(mesh):
    placed = (
        P("dp", "mp", None),
        P("dp", None),
        P("dp", "mp", None),
        P(None, None, "mp"),
        P(None, "mp"),
        P(None, None, "mp"),
        P(None, None, "mp"),
        P(None, "mp"),
        P(None, None, "mp"),
        P(),
        P(),
        P(),
        P(None, None, "mp"),
        P(None, "mp"),
        P(None, None, "mp"),
        P(),
        P(),
        P(),
    )
    return jax.shard_map(
        shards,
        mesh=mesh,
        in_specs=placed,
        out_specs=(
            P("dp", "mp", None),
            P("dp", "mp", None),
            P(None, "dp", "mp"),
            P(None, "mp"),
            P(None, "dp", "mp"),
            P(None, "dp", "mp"),
            P(None, "mp"),
            P(None, "dp", "mp"),
            P(),
            P(),
            P(),
            P(None, "dp", "mp"),
            P(None, "mp"),
            P(None, "dp", "mp"),
            P(),
            P(),
            P(),
        ),
        check_vma=False,
    )
```

profile of v0, /device:TPU:0, one launch (start us, length us, event | category | flops | bytes accessed | tf_op | source)
XLA Modules:
  0.0 1289.5 jit_solution(6457793700679230937)
XLA Ops:
  13.4 8.7 all-gather.11.cloned.1.call-done
  37.4 24.5 %while.72 = (s32[]{:T(128)}, bf16[2,512,384]{1,2,0:T(8,128)(2,1)}, bf16[2,512,384]{1,2,0:T(8,128)(2,1)S(1)}, pred[2,512,512]{1,2,0:T(8,128)(4,1)S(1)}, bf16[2,51...) while((s32[]{:T(128)}, bf16[2,512,384]{1,2,0:T(8,128)(2,1)}, ...), condition=%wide.region_4.5_spmd, body=%wide.region_1.4_spmd.sunk | while | flops 412287488 | bytes 24404124 | solution.py:120
  38.4 6.8 fusion.329
  50.7 6.8 fusion.329
  66.9 11.2 while.76
  86.1 7.5 reduce-scatter.32.cloned.1.call-done
  97.7 10.5 all-gather.13.cloned.1.call-done
  108.1 9.2 fusion.93
  118.6 9.1 reduce-scatter.18.cloned.1.call-done
  132.6 11.1 all-gather.25.cloned.1.call-done
  143.7 6.6 multiply_convert_fusion.2
  151.9 5.4 fusion.96
  158.6 9.1 reduce-scatter.34.cloned.1.call-done
  167.7 4.9 fusion.183
  172.7 11.1 all-gather.15.cloned.1.call-done
  198.1 22.5 %while.73 = (s32[]{:T(128)}, bf16[2,512,384]{1,2,0:T(8,128)(2,1)}, bf16[2,512,384]{1,2,0:T(8,128)(2,1)S(1)}, pred[2,512,512]{1,2,0:T(8,128)(4,1)S(1)}, bf16[2,51...) while((s32[]{:T(128)}, bf16[2,512,384]{1,2,0:T(8,128)(2,1)}, ...), condition=%wide.region_14.15_spmd, body=%wide.region_11.14_spmd.sunk | while | flops 412287488 | bytes 24404124 | solution.py:120
  199.2 5.7 fusion.334
  210.5 5.7 fusion.334
  224.7 11.4 while.74
  242.3 8.7 reduce-scatter.24.cloned.1.call-done
  254.5 11.1 all-gather.17.cloned.1.call-done
  265.6 9.2 fusion.102
  275.1 10.2 reduce-scatter.22.cloned.1.call-done
  289.3 11.1 all-gather.19.cloned.1.call-done
  300.4 6.6 multiply_convert_fusion.3
  308.6 5.5 fusion.105
  314.1 10.3 reduce-scatter.26.cloned.1.call-done
  332.3 11.1 all-gather.21.cloned.1.call-done
  343.4 8.0 convert_reduce_fusion
  353.1 5.4 fusion.99
  358.6 10.3 reduce-scatter.28.cloned.1.call-done
  377.2 10.9 all-gather.23.cloned.1.call-done
  393.5 30.1 %while.75 = (s32[]{:T(128)}, bf16[2,512,384]{1,2,0:T(8,128)(2,1)}, bf16[2,512,384]{1,2,0:T(8,128)(2,1)}, bf16[2,512,384]{1,2,0:T(8,128)(2,1)}, bf16[2,512,384]{1...) while((s32[]{:T(128)}, bf16[2,512,384]{1,2,0:T(8,128)(2,1)}, ...), condition=%wide.region_38.39_spmd, body=%wide.region_36.38_spmd.sunk | while | flops 1031205888 | bytes 93606456 | solution.py:221
  431.6 8.7 reduce-scatter.30.cloned.1.call-done
  447.4 11.1 all-gather.27.cloned.1.call-done
  458.5 8.2 convert_reduce_fusion.1
  472.3 10.3 reduce-scatter.36.cloned.1.call-done
  488.9 11.0 all-gather.29.cloned.1.call-done
  505.1 32.2 %while.77 = (s32[]{:T(128)}, bf16[2,512,384]{1,2,0:T(8,128)(2,1)}, bf16[2,512,384]{1,2,0:T(8,128)(2,1)}, bf16[2,512,384]{1,2,0:T(8,128)(2,1)}, bf16[2,512,384]{1...) while((s32[]{:T(128)}, bf16[2,512,384]{1,2,0:T(8,128)(2,1)}, ...), condition=%wide.region_57.58_spmd, body=%wide.region_55.57_spmd.sunk | while | flops 1031205888 | bytes 87118264 | solution.py:221
  574.3 4.7 convolution_bitcast_fusion
  586.5 5.2 convolution_bitcast_fusion.2
  594.4 4.5 pad_maximum_fusion
  605.9 43.8 %all-reduce.3 = (f32[2,768]{1,0:T(2,128)}, f32[2,768]{1,0:T(2,128)}, f32[2,768]{1,0:T(2,128)}, f32[2,768]{1,0:T(2,128)}, f32[2,768]{1,0:T(2,128)}, /*index=5*/f32[2,768]{1,0:T(2,128)}) all-reduce(f32[2,768]{1,0:T(2,128)S(1)} %pad_maximum_fusion.7, f32[2,768]{1,0:T(2,128)S(1)} %pad_maximum_fusion.8, ...), channel_id=1, replica_groups=mesh['dp'=16,'mp'=2] {'dp','mp'}, use_global_device_ids=true, to_apply=%region_71.72 | all-reduce | flops 9216 | bytes 73728 | tf_op jit(solution)/shard_map/psum | solution.py:331
  650.2 76.6 %all-reduce.4 = (f32[2,384]{1,0:T(2,128)}, f32[2,384]{1,0:T(2,128)}, f32[2,1536]{1,0:T(2,128)}) all-reduce(f32[2,384]{1,0:T(2,128)S(1)} %pad_maximum_fusion.13, f32[2,384]{1,0:T(2,128)S(1)} %pad_maximum_fusion.14, f32[2,1536]{1,0:T(2,128)S(1)} %pad_maximum_fusion.6), channel_id=1, replica_groups=mesh['dp'=16,'mp'=2] {'dp'}, use_global_device_ids=true, to_apply=%region_62.63 | all-reduce | flops 4608 | bytes 36864 | tf_op jit(solution)/shard_map/psum | solution.py:330
  729.2 68.2 %all-reduce.8.cloned.1.call-done = (f32[2,768,384]{2,0,1:T(2,128)}, f32[2,768,384]{2,0,1:T(2,128)}, f32[2,768,384]{2,0,1:T(2,128)}) async-done(((f32[2,768,384]{2,0,1:T(2,128)}, f32[2,768,384]{2,0,1:T(2,128)}, f32[2,768,384]{2,0,1:T(2,128)}), (f32[2,768,384]{2,0,1:T(2,128)}, f32[2,768,384]{2,0,1:T(2,128)}, f32[2,768,384]{2,0,1:T(2,128)})) %all-reduce.8.cloned.1.call-update) | async-done | bytes 7077904
  802.3 127.2 %reduce-scatter.40.cloned.1.call-done = f32[2,48,384]{2,1,0:T(8,128)} async-done(((f32[2,768,384]{2,1,0:T(8,128)}), f32[2,48,384]{2,1,0:T(8,128)}) %reduce-scatter.40.cloned.1.call-update) | async-done | bytes 147472 | tf_op jit(solution)/shard_map/reduce_scatter | solution.py:326
  929.5 177.2 %reduce-scatter.44.cloned.1.call-done = f32[2,48,1536]{2,1,0:T(8,128)} async-done(((f32[2,768,1536]{2,1,0:T(8,128)}), f32[2,48,1536]{2,1,0:T(8,128)}) %reduce-scatter.44.cloned.1.call-update) | async-done | bytes 589840 | tf_op jit(solution)/shard_map/reduce_scatter | solution.py:328
  1106.7 175.9 %reduce-scatter.42.cloned.1.call-done = f32[2,48,1536]{2,1,0:T(8,128)} async-done(((f32[2,768,1536]{2,1,0:T(8,128)}), f32[2,48,1536]{2,1,0:T(8,128)}) %reduce-scatter.42.cloned.1.call-update) | async-done | bytes 589840 | tf_op jit(solution)/shard_map/reduce_scatter | solution.py:327
  (688 shorter events, 302.6 us)
Async XLA Ops:
  7.2 14.9 %all-gather.11.cloned.1.call-start = ((), (), s32[]{:S(2)}) async-start(), calls=%async_computation.15 | async-start | bytes 2359296 | tf_op jit(solution)/shard_map/all_gather | solution.py:116
  7.9 76.6 %reduce-scatter.16.cloned.1.call-start = ((), (), s32[]{:S(2)}) async-start(), calls=%async_computation.16 | async-start | bytes 2359296 | tf_op jit(solution)/shard_map/reduce_scatter | solution.py:122
  65.4 28.1 %reduce-scatter.32.cloned.1.call-start = ((), (), s32[]{:S(2)}) async-start(), calls=%async_computation.30 | async-start | bytes 2359296 | tf_op jit(solution)/shard_map/reduce_scatter | solution.py:122
  83.2 24.9 %all-gather.13.cloned.1.call-start = ((), (), s32[]{:S(2)}) async-start(), calls=%async_computation.17 | async-start | bytes 2359296 | tf_op jit(solution)/shard_map/all_gather | solution.py:129
  83.9 83.8 %copy-start.86 = (f32[768]{0:T(1024)}, f32[768]{0:T(1024)S(1)}, u32[]{:S(2)}) copy-start(f32[768]{0:T(1024)S(1)} %get-tuple-element.490) | copy-start | bytes 9220
  84.5 83.2 %copy-start.94 = (f32[768]{0:T(1024)}, f32[768]{0:T(1024)S(1)}, u32[]{:S(2)}) copy-start(f32[768]{0:T(1024)S(1)} %get-tuple-element.664) | copy-start | bytes 9220
  97.0 30.8 %reduce-scatter.18.cloned.1.call-start = ((), (), s32[]{:S(2)}) async-start(), calls=%async_computation.18 | async-start | bytes 2359296 | tf_op jit(solution)/shard_map/reduce_scatter | solution.py:133
  97.7 46.0 %copy-start.137 = (f32[1536]{0:T(1024)}, f32[1536]{0:T(1024)S(1)}, u32[]{:S(2)}) copy-start(f32[1536]{0:T(1024)S(1)} %get-tuple-element.488) | copy-start | bytes 18436
  117.4 12.4 copy-start.12
  117.4 26.3 %all-gather.25.cloned.1.call-start = ((), (), s32[]{:S(2)}) async-start(), calls=%async_computation.31 | async-start | bytes 2359296 | tf_op jit(solution)/shard_map/all_gather | solution.py:129
  118.6 49.1 %copy-start.102 = (f32[2,256]{1,0:T(2,128)}, f32[2,256]{1,0:T(2,128)S(1)}, u32[]{:S(2)}) copy-start(f32[2,256]{1,0:T(2,128)S(1)} %broadcast_multiply_fusion.1) | copy-start | bytes 6148
  131.1 36.6 %copy-start.110 = (f32[2,256]{1,0:T(2,128)}, f32[2,256]{1,0:T(2,128)S(1)}, u32[]{:S(2)}) copy-start(f32[2,256]{1,0:T(2,128)S(1)} %fusion.166) | copy-start | bytes 6148
  132.5 35.2 %reduce-scatter.34.cloned.1.call-start = ((), (), s32[]{:S(2)}) async-start(), calls=%async_computation.32 | async-start | bytes 2359296 | tf_op jit(solution)/shard_map/reduce_scatter | solution.py:133
  157.3 26.5 %all-gather.15.cloned.1.call-start = ((), (), s32[]{:S(2)}) async-start(), calls=%async_computation.19 | async-start | bytes 2359296 | tf_op jit(solution)/shard_map/all_gather | solution.py:116
  158.6 14.0 %copy-start.108 = (f32[768]{0:T(1024)}, f32[768]{0:T(1024)S(1)}, u32[]{:S(2)}) copy-start(f32[768]{0:T(1024)S(1)} %get-tuple-element.667) | copy-start | bytes 9220
  167.7 16.1 %copy-start.143 = (f32[384]{0:T(512)S(1)}, f32[384]{0:T(512)}, u32[]{:S(2)}) copy-start(f32[384]{0:T(512)} %get-tuple-element.501) | copy-start | bytes 4612
  172.7 68.0 %reduce-scatter.20.cloned.1.call-start = ((), (), s32[]{:S(2)}) async-start(), calls=%async_computation.20 | async-start | bytes 2359296 | tf_op jit(solution)/shard_map/reduce_scatter | solution.py:122
  224.2 26.8 %reduce-scatter.24.cloned.1.call-start = ((), (), s32[]{:S(2)}) async-start(), calls=%async_computation.23 | async-start | bytes 2359296 | tf_op jit(solution)/shard_map/reduce_scatter | solution.py:122
  240.6 25.0 %all-gather.17.cloned.1.call-start = ((), (), s32[]{:S(2)}) async-start(), calls=%async_computation.21 | async-start | bytes 2359296 | tf_op jit(solution)/shard_map/all_gather | solution.py:129
  242.3 10.8 copy-start.98
  242.3 126.6 %copy-start.104 = (f32[2,256]{1,0:T(2,128)}, f32[2,256]{1,0:T(2,128)S(1)}, u32[]{:S(2)}) copy-start(f32[2,256]{1,0:T(2,128)S(1)} %broadcast_multiply_fusion.5) | copy-start | bytes 6148
  253.0 115.9 %copy-start.112 = (f32[2,256]{1,0:T(2,128)}, f32[2,256]{1,0:T(2,128)S(1)}, u32[]{:S(2)}) copy-start(f32[2,256]{1,0:T(2,128)S(1)} %add_rsqrt_fusion.1) | copy-start | bytes 6148
  253.0 12.6 copy-start.139
  254.4 30.8 %reduce-scatter.22.cloned.1.call-start = ((), (), s32[]{:S(2)}) async-start(), calls=%async_computation.22 | async-start | bytes 2359296 | tf_op jit(solution)/shard_map/reduce_scatter | solution.py:133
  274.9 25.5 %all-gather.19.cloned.1.call-start = ((), (), s32[]{:S(2)}) async-start(), calls=%async_computation.24 | async-start | bytes 2359296 | tf_op jit(solution)/shard_map/all_gather | solution.py:129
  289.2 35.2 %reduce-scatter.26.cloned.1.call-start = ((), (), s32[]{:S(2)}) async-start(), calls=%async_computation.25 | async-start | bytes 2359296 | tf_op jit(solution)/shard_map/reduce_scatter | solution.py:133
  314.1 29.3 %all-gather.21.cloned.1.call-start = ((), (), s32[]{:S(2)}) async-start(), calls=%async_computation.26 | async-start | bytes 2359296 | tf_op jit(solution)/shard_map/all_gather | solution.py:193
  332.2 36.7 %reduce-scatter.28.cloned.1.call-start = ((), (), s32[]{:S(2)}) async-start(), calls=%async_computation.27 | async-start | bytes 2359296 | tf_op jit(solution)/shard_map/reduce_scatter | solution.py:205
  358.5 29.6 %all-gather.23.cloned.1.call-start = ((), (), s32[]{:S(2)}) async-start(), calls=%async_computation.28 | async-start | bytes 2359296 | tf_op jit(solution)/shard_map/all_gather | solution.py:214
  358.6 14.5 %copy-start.115 = (f32[2,256]{1,0:T(2,128)}, f32[2,256]{1,0:T(2,128)S(1)}, u32[]{:S(2)}) copy-start(f32[2,256]{1,0:T(2,128)S(1)} %broadcast_multiply_fusion.4) | copy-start | bytes 6148
  377.0 63.3 %reduce-scatter.30.cloned.1.call-start = ((), (), s32[]{:S(2)}) async-start(), calls=%async_computation.29 | async-start | bytes 2359296 | tf_op jit(solution)/shard_map/reduce_scatter | solution.py:240
  429.9 28.7 %all-gather.27.cloned.1.call-start = ((), (), s32[]{:S(2)}) async-start(), calls=%async_computation.33 | async-start | bytes 2359296 | tf_op jit(solution)/shard_map/all_gather | solution.py:193
  443.6 24.8 %slice-start = ((s8[4718592]{0:T(1024)(128)(4,1)}), s8[524288]{0:T(1024)(128)(4,1)S(1)}, s32[]{:S(2)}) async-start(s8[4718592]{0:T(1024)(128)(4,1)} %bitcast.486), calls=%async_computation.41 | async-start | bytes 1048576
  445.7 12.9 copy-start.138
  447.4 35.2 %reduce-scatter.36.cloned.1.call-start = ((), (), s32[]{:S(2)}) async-start(), calls=%async_computation.34 | async-start | bytes 2359296 | tf_op jit(solution)/shard_map/reduce_scatter | solution.py:205
  468.4 14.2 %copy-start.87 = (f32[768]{0:T(1024)S(1)}, f32[768]{0:T(1024)}, u32[]{:S(2)}) copy-start(f32[768]{0:T(1024)} %copy-done.86) | copy-start | bytes 9220
  468.4 14.2 %copy-start.95 = (f32[768]{0:T(1024)S(1)}, f32[768]{0:T(1024)}, u32[]{:S(2)}) copy-start(f32[768]{0:T(1024)} %copy-done.94) | copy-start | bytes 9220
  468.4 14.2 %copy-start.111 = (f32[2,256]{1,0:T(2,128)S(1)}, f32[2,256]{1,0:T(2,128)}, u32[]{:S(2)}) copy-start(f32[2,256]{1,0:T(2,128)} %copy-done.110) | copy-start | bytes 6148
  472.2 13.2 %copy-start.118 = (f32[2,256]{1,0:T(2,128)S(1)}, f32[2,256]{1,0:T(2,128)}, u32[]{:S(2)}) copy-start(f32[2,256]{1,0:T(2,128)} %copy-done.117) | copy-start | bytes 6148
  472.2 27.7 %all-gather.29.cloned.1.call-start = ((), (), s32[]{:S(2)}) async-start(), calls=%async_computation.35 | async-start | bytes 2359296 | tf_op jit(solution)/shard_map/all_gather | solution.py:214
  487.6 12.3 copy-start.147
  488.7 238.0 %reduce-scatter.38.cloned.1.call-start = ((), (), s32[]{:S(2)}) async-start(), calls=%async_computation.36 | async-start | bytes 2359296 | tf_op jit(solution)/shard_map/reduce_scatter | solution.py:240
  543.5 253.9 %all-reduce.8.cloned.1.call-start = ((), (), s32[]{:S(2)}) async-start(), calls=%async_computation.40 | async-start | bytes 14155776
  566.2 363.3 %reduce-scatter.40.cloned.1.call-start = ((), (), s32[]{:S(2)}) async-start(), calls=%async_computation.37 | async-start | bytes 2506752 | tf_op jit(solution)/shard_map/reduce_scatter | solution.py:326
  572.5 534.2 %reduce-scatter.44.cloned.1.call-start = ((), (), s32[]{:S(2)}) async-start(), calls=%async_computation.39 | async-start | bytes 10027008 | tf_op jit(solution)/shard_map/reduce_scatter | solution.py:328
  586.2 696.3 %reduce-scatter.42.cloned.1.call-start = ((), (), s32[]{:S(2)}) async-start(), calls=%async_computation.38 | async-start | bytes 10027008 | tf_op jit(solution)/shard_map/reduce_scatter | solution.py:327
  605.0 121.7 %copy-start.26 = (f32[2,256,768]{2,1,0:T(8,128)S(1)}, f32[2,256,768]{2,1,0:T(8,128)}, u32[]{:S(2)}) copy-start(f32[2,256,768]{2,1,0:T(8,128)} %copy-done.25) | copy-start | bytes 4718596
  605.2 44.7 %copy-start.40 = (bf16[2,512,384]{1,2,0:T(8,128)(2,1)S(1)}, bf16[2,512,384]{1,2,0:T(8,128)(2,1)}, u32[]{:S(2)}) copy-start(bf16[2,512,384]{1,2,0:T(8,128)(2,1)} %get-tuple-element.274) | copy-start | bytes 2359300
  (159 other events, 412.5 us)
Sparse Core Ops, SparseCore 0:
  9.6 12.4 all-gather.10
  65.6 10.2 reduce-scatter.15
  83.3 10.2 reduce-scatter.31
  97.1 10.9 all-gather.12
  117.5 10.2 reduce-scatter.17
  132.6 10.9 all-gather.24
  157.4 10.2 reduce-scatter.33
  172.8 10.9 all-gather.14
  224.3 10.3 reduce-scatter.19
  240.7 10.2 reduce-scatter.23
  254.5 11.0 all-gather.16
  275.0 10.2 reduce-scatter.21
  289.4 10.9 all-gather.18
  314.2 10.2 reduce-scatter.25
  332.3 10.9 all-gather.20
  358.6 10.2 reduce-scatter.27
  377.1 10.9 all-gather.22
  430.0 10.2 reduce-scatter.29
  447.5 10.9 all-gather.26
  472.3 10.1 reduce-scatter.35
  488.8 11.0 all-gather.28
  543.6 10.2 reduce-scatter.37
  566.3 231.1 all-reduce.7
  802.8 126.6 reduce-scatter.39
  936.7 169.9 reduce-scatter.43
  1112.8 169.7 reduce-scatter.41
where the time goes:
time: 1300 us; the launch traced here: 1290 us
  waiting for transfers between devices  741 us (57%)
  matrix products  229 us (18%)
  blocking collectives  120 us (9%)
  local copies, waits for them, and re-layouts  90.8 us (7%)
  other arithmetic  86.7 us (7%)
  between operations  16.8 us (1%)
    reduce_scatter x1, waiting for transfers between devices, shards(): lax.psum_scatter(stacked[11], 'dp', scatter_dimension=1, tiled=True)  177 us
    reduce_scatter x1, waiting for transfers between devices, shards(): lax.psum_scatter(stacked[9], 'dp', scatter_dimension=1, tiled=True)  176 us
    reduce_scatter x1, waiting for transfers between devices, shards(): lax.psum_scatter(stacked[5], 'dp', scatter_dimension=1, tiled=True)  127 us
    psum x1, blocking collectives, shards(): columns = lax.psum((stacked[1], stacked[4], stacked[10]), 'dp')  76.6 us
    unnamed x27, waiting for transfers between devices  69.3 us
    psum x1, blocking collectives, shards(): lax.psum((stacked[6], stacked[7], stacked[8], stacked[12], stacked[13], s...  43.8 us
    all_gather x4, waiting for transfers between devices, forward_layer(): lax.all_gather(normed.astype(jnp.bfloat16), 'mp', axis=1, tiled=True)  43.8 us
    reduce_scatter x4, waiting for transfers between devices, forward_layer(): lax.psum_scatter(partial_down.astype(jnp.bfloat16), 'mp', scatter_dimensi...  38.7 us
  transfers between devices with their start and end apart: 26, of which 23 were waited for; matrix products, arithmetic and copies ran while one was open for 8% of the time, Pallas kernels for 0%

commit v1 on v0

--- a/solution.py
+++ b/solution.py
@@ -328,9 +328,8 @@
         lax.psum_scatter(stacked[11], "dp", scatter_dimension=1, tiled=True),
     )
     columns = lax.psum((stacked[1], stacked[4], stacked[10]), "dp")
-    rows_summed = lax.psum(
-        (stacked[6], stacked[7], stacked[8], stacked[12], stacked[13], stacked[14]), ("dp", "mp")
-    )
+    mat = (stacked[6], stacked[7], stacked[8], stacked[12], stacked[13], stacked[14])
+    rows_summed = jax.lax.psum(jax.lax.psum(mat, "dp"), "mp")
     return (
         hidden,
         grad_hidden,

time: 1300 us -> 1300 us (level)
  blocking collectives: 120 us -> 82.8 us
  waiting for transfers between devices: 741 us -> 778 us
    psum x1, blocking collectives: 43.8 us -> 4.03 us  [shards(): rows_summed = jax.lax.psum(jax.lax.psum(mat, 'dp'), 'mp')]
    unnamed x27, waiting for transfers between devices: 69.3 us -> 106 us
where the time goes in v1:
time: 1300 us; the launch traced here: 1290 us
  waiting for transfers between devices  778 us (60%)
  matrix products  229 us (18%)
  local copies, waits for them, and re-layouts  90.8 us (7%)
  other arithmetic  86.7 us (7%)
  blocking collectives  82.8 us (6%)
  between operations  16.8 us (1%)
    reduce_scatter x1, waiting for transfers between devices, shards(): lax.psum_scatter(stacked[11], 'dp', scatter_dimension=1, tiled=True)  177 us
    reduce_scatter x1, waiting for transfers between devices, shards(): lax.psum_scatter(stacked[9], 'dp', scatter_dimension=1, tiled=True)  176 us
    reduce_scatter x1, waiting for transfers between devices, shards(): lax.psum_scatter(stacked[5], 'dp', scatter_dimension=1, tiled=True)  127 us
    unnamed x27, waiting for transfers between devices  106 us
    psum x1, blocking collectives, shards(): columns = lax.psum((stacked[1], stacked[4], stacked[10]), 'dp')  78.8 us
    all_gather x4, waiting for transfers between devices, forward_layer(): lax.all_gather(normed.astype(jnp.bfloat16), 'mp', axis=1, tiled=True)  43.8 us
    reduce_scatter x4, waiting for transfers between devices, forward_layer(): lax.psum_scatter(partial_down.astype(jnp.bfloat16), 'mp', scatter_dimensi...  38.7 us
    dot_general x8, matrix products, project(): jnp.einsum('rsd,de->rse', left, right, preferred_element_type=jnp.float32)  32.4 us
  transfers between devices with their start and end apart: 26, of which 23 were waited for; matrix products, arithmetic and copies ran while one was open for 8% of the time, Pallas kernels for 0%

profile of v1, /device:TPU:0, one launch (start us, length us, event | category | flops | bytes accessed | tf_op | source)
XLA Modules:
  0.0 1288.9 jit_solution(9016008682052493631)
XLA Ops:
  13.4 8.7 all-gather.11.cloned.1.call-done
  37.4 24.5 %while.72 = (s32[]{:T(128)}, bf16[2,512,384]{1,2,0:T(8,128)(2,1)}, bf16[2,512,384]{1,2,0:T(8,128)(2,1)S(1)}, pred[2,512,512]{1,2,0:T(8,128)(4,1)S(1)}, bf16[2,51...) while((s32[]{:T(128)}, bf16[2,512,384]{1,2,0:T(8,128)(2,1)}, ...), condition=%wide.region_4.5_spmd, body=%wide.region_1.4_spmd.sunk | while | flops 412287488 | bytes 24404124 | solution.py:120
  38.4 6.8 fusion.329
  50.7 6.8 fusion.329
  66.9 11.2 while.76
  86.1 7.5 reduce-scatter.32.cloned.1.call-done
  97.7 10.5 all-gather.13.cloned.1.call-done
  108.1 9.2 fusion.93
  118.6 9.1 reduce-scatter.18.cloned.1.call-done
  132.6 11.1 all-gather.25.cloned.1.call-done
  143.7 6.6 multiply_convert_fusion.2
  151.9 5.4 fusion.96
  158.6 9.1 reduce-scatter.34.cloned.1.call-done
  167.7 4.9 fusion.183
  172.7 11.1 all-gather.15.cloned.1.call-done
  198.1 22.5 %while.73 = (s32[]{:T(128)}, bf16[2,512,384]{1,2,0:T(8,128)(2,1)}, bf16[2,512,384]{1,2,0:T(8,128)(2,1)S(1)}, pred[2,512,512]{1,2,0:T(8,128)(4,1)S(1)}, bf16[2,51...) while((s32[]{:T(128)}, bf16[2,512,384]{1,2,0:T(8,128)(2,1)}, ...), condition=%wide.region_14.15_spmd, body=%wide.region_11.14_spmd.sunk | while | flops 412287488 | bytes 24404124 | solution.py:120
  199.2 5.7 fusion.334
  210.5 5.7 fusion.334
  224.7 11.4 while.74
  242.3 8.7 reduce-scatter.24.cloned.1.call-done
  254.5 11.1 all-gather.17.cloned.1.call-done
  265.6 9.2 fusion.102
  275.1 10.2 reduce-scatter.22.cloned.1.call-done
  289.3 11.1 all-gather.19.cloned.1.call-done
  300.4 6.6 multiply_convert_fusion.3
  308.6 5.5 fusion.105
  314.1 10.3 reduce-scatter.26.cloned.1.call-done
  332.3 11.1 all-gather.21.cloned.1.call-done
  343.4 8.0 convert_reduce_fusion
  353.1 5.4 fusion.99
  358.6 10.3 reduce-scatter.28.cloned.1.call-done
  377.2 10.9 all-gather.23.cloned.1.call-done
  393.5 30.1 %while.75 = (s32[]{:T(128)}, bf16[2,512,384]{1,2,0:T(8,128)(2,1)}, bf16[2,512,384]{1,2,0:T(8,128)(2,1)}, bf16[2,512,384]{1,2,0:T(8,128)(2,1)}, bf16[2,512,384]{1...) while((s32[]{:T(128)}, bf16[2,512,384]{1,2,0:T(8,128)(2,1)}, ...), condition=%wide.region_38.39_spmd, body=%wide.region_36.38_spmd.sunk | while | flops 1031205888 | bytes 93606456 | solution.py:221
  431.6 8.7 reduce-scatter.30.cloned.1.call-done
  447.4 11.1 all-gather.27.cloned.1.call-done
  458.5 8.2 convert_reduce_fusion.1
  472.3 10.3 reduce-scatter.36.cloned.1.call-done
  488.9 11.0 all-gather.29.cloned.1.call-done
  505.1 32.2 %while.77 = (s32[]{:T(128)}, bf16[2,512,384]{1,2,0:T(8,128)(2,1)}, bf16[2,512,384]{1,2,0:T(8,128)(2,1)}, bf16[2,512,384]{1,2,0:T(8,128)(2,1)}, bf16[2,512,384]{1...) while((s32[]{:T(128)}, bf16[2,512,384]{1,2,0:T(8,128)(2,1)}, ...), condition=%wide.region_57.58_spmd, body=%wide.region_55.57_spmd.sunk | while | flops 1031205888 | bytes 87118264 | solution.py:221
  574.3 4.7 convolution_bitcast_fusion
  581.7 4.5 pad_maximum_fusion.1
  586.5 5.2 convolution_bitcast_fusion.2
  594.4 4.5 pad_maximum_fusion
  606.4 78.8 %all-reduce.3 = (f32[2,384]{1,0:T(2,128)}, f32[2,384]{1,0:T(2,128)}, f32[2,768]{1,0:T(2,128)S(1)}, f32[2,768]{1,0:T(2,128)S(1)}, f32[2,768]{1,0:T(2,128)S(1)}, /...) all-reduce(f32[2,384]{1,0:T(2,128)S(1)} %pad_maximum_fusion.13, ...), channel_id=1, replica_groups=mesh['dp'=16,'mp'=2] {'dp'}, use_global_device_ids=true, to_apply=%region_62.63 | all-reduce | flops 13824 | bytes 110592 | tf_op jit(solution)/shard_map/psum | solution.py:330
  691.7 105.1 %all-reduce.8.cloned.1.call-done = (f32[2,768,384]{2,0,1:T(2,128)}, f32[2,768,384]{2,0,1:T(2,128)}, f32[2,768,384]{2,0,1:T(2,128)}) async-done(((f32[2,768,384]{2,0,1:T(2,128)}, f32[2,768,384]{2,0,1:T(2,128)}, f32[2,768,384]{2,0,1:T(2,128)}), (f32[2,768,384]{2,0,1:T(2,128)}, f32[2,768,384]{2,0,1:T(2,128)}, f32[2,768,384]{2,0,1:T(2,128)})) %all-reduce.8.cloned.1.call-update) | async-done | bytes 7077904
  801.7 127.2 %reduce-scatter.40.cloned.1.call-done = f32[2,48,384]{2,1,0:T(8,128)} async-done(((f32[2,768,384]{2,1,0:T(8,128)}), f32[2,48,384]{2,1,0:T(8,128)}) %reduce-scatter.40.cloned.1.call-update) | async-done | bytes 147472 | tf_op jit(solution)/shard_map/reduce_scatter | solution.py:326
  928.9 177.2 %reduce-scatter.44.cloned.1.call-done = f32[2,48,1536]{2,1,0:T(8,128)} async-done(((f32[2,768,1536]{2,1,0:T(8,128)}), f32[2,48,1536]{2,1,0:T(8,128)}) %reduce-scatter.44.cloned.1.call-update) | async-done | bytes 589840 | tf_op jit(solution)/shard_map/reduce_scatter | solution.py:328
  1106.1 175.9 %reduce-scatter.42.cloned.1.call-done = f32[2,48,1536]{2,1,0:T(8,128)} async-done(((f32[2,768,1536]{2,1,0:T(8,128)}), f32[2,48,1536]{2,1,0:T(8,128)}) %reduce-scatter.42.cloned.1.call-update) | async-done | bytes 589840 | tf_op jit(solution)/shard_map/reduce_scatter | solution.py:327
  (688 shorter events, 302.2 us)
Async XLA Ops:
  7.2 14.9 %all-gather.11.cloned.1.call-start = ((), (), s32[]{:S(2)}) async-start(), calls=%async_computation.15 | async-start | bytes 2359296 | tf_op jit(solution)/shard_map/all_gather | solution.py:116
  7.9 76.6 %reduce-scatter.16.cloned.1.call-start = ((), (), s32[]{:S(2)}) async-start(), calls=%async_computation.16 | async-start | bytes 2359296 | tf_op jit(solution)/shard_map/reduce_scatter | solution.py:122
  65.4 28.1 %reduce-scatter.32.cloned.1.call-start = ((), (), s32[]{:S(2)}) async-start(), calls=%async_computation.30 | async-start | bytes 2359296 | tf_op jit(solution)/shard_map/reduce_scatter | solution.py:122
  83.2 24.9 %all-gather.13.cloned.1.call-start = ((), (), s32[]{:S(2)}) async-start(), calls=%async_computation.17 | async-start | bytes 2359296 | tf_op jit(solution)/shard_map/all_gather | solution.py:129
  83.9 83.8 %copy-start.86 = (f32[768]{0:T(1024)}, f32[768]{0:T(1024)S(1)}, u32[]{:S(2)}) copy-start(f32[768]{0:T(1024)S(1)} %get-tuple-element.490) | copy-start | bytes 9220
  84.5 83.2 %copy-start.94 = (f32[768]{0:T(1024)}, f32[768]{0:T(1024)S(1)}, u32[]{:S(2)}) copy-start(f32[768]{0:T(1024)S(1)} %get-tuple-element.670) | copy-start | bytes 9220
  97.0 30.8 %reduce-scatter.18.cloned.1.call-start = ((), (), s32[]{:S(2)}) async-start(), calls=%async_computation.18 | async-start | bytes 2359296 | tf_op jit(solution)/shard_map/reduce_scatter | solution.py:133
  97.7 46.0 %copy-start.137 = (f32[1536]{0:T(1024)}, f32[1536]{0:T(1024)S(1)}, u32[]{:S(2)}) copy-start(f32[1536]{0:T(1024)S(1)} %get-tuple-element.488) | copy-start | bytes 18436
  117.4 12.4 copy-start.12
  117.4 26.3 %all-gather.25.cloned.1.call-start = ((), (), s32[]{:S(2)}) async-start(), calls=%async_computation.31 | async-start | bytes 2359296 | tf_op jit(solution)/shard_map/all_gather | solution.py:129
  118.6 49.1 %copy-start.102 = (f32[2,256]{1,0:T(2,128)}, f32[2,256]{1,0:T(2,128)S(1)}, u32[]{:S(2)}) copy-start(f32[2,256]{1,0:T(2,128)S(1)} %broadcast_multiply_fusion.1) | copy-start | bytes 6148
  131.1 36.6 %copy-start.110 = (f32[2,256]{1,0:T(2,128)}, f32[2,256]{1,0:T(2,128)S(1)}, u32[]{:S(2)}) copy-start(f32[2,256]{1,0:T(2,128)S(1)} %fusion.166) | copy-start | bytes 6148
  132.5 35.2 %reduce-scatter.34.cloned.1.call-start = ((), (), s32[]{:S(2)}) async-start(), calls=%async_computation.32 | async-start | bytes 2359296 | tf_op jit(solution)/shard_map/reduce_scatter | solution.py:133
  157.3 26.5 %all-gather.15.cloned.1.call-start = ((), (), s32[]{:S(2)}) async-start(), calls=%async_computation.19 | async-start | bytes 2359296 | tf_op jit(solution)/shard_map/all_gather | solution.py:116
  158.6 14.0 %copy-start.108 = (f32[768]{0:T(1024)}, f32[768]{0:T(1024)S(1)}, u32[]{:S(2)}) copy-start(f32[768]{0:T(1024)S(1)} %get-tuple-element.673) | copy-start | bytes 9220
  167.7 16.1 %copy-start.143 = (f32[384]{0:T(512)S(1)}, f32[384]{0:T(512)}, u32[]{:S(2)}) copy-start(f32[384]{0:T(512)} %get-tuple-element.501) | copy-start | bytes 4612
  172.7 68.0 %reduce-scatter.20.cloned.1.call-start = ((), (), s32[]{:S(2)}) async-start(), calls=%async_computation.20 | async-start | bytes 2359296 | tf_op jit(solution)/shard_map/reduce_scatter | solution.py:122
  224.2 26.8 %reduce-scatter.24.cloned.1.call-start = ((), (), s32[]{:S(2)}) async-start(), calls=%async_computation.23 | async-start | bytes 2359296 | tf_op jit(solution)/shard_map/reduce_scatter | solution.py:122
  240.6 25.0 %all-gather.17.cloned.1.call-start = ((), (), s32[]{:S(2)}) async-start(), calls=%async_computation.21 | async-start | bytes 2359296 | tf_op jit(solution)/shard_map/all_gather | solution.py:129
  242.3 10.8 copy-start.96
  242.3 10.8 copy-start.98
  242.3 126.6 %copy-start.104 = (f32[2,256]{1,0:T(2,128)}, f32[2,256]{1,0:T(2,128)S(1)}, u32[]{:S(2)}) copy-start(f32[2,256]{1,0:T(2,128)S(1)} %broadcast_multiply_fusion.5) | copy-start | bytes 6148
  253.0 115.9 %copy-start.112 = (f32[2,256]{1,0:T(2,128)}, f32[2,256]{1,0:T(2,128)S(1)}, u32[]{:S(2)}) copy-start(f32[2,256]{1,0:T(2,128)S(1)} %add_rsqrt_fusion.1) | copy-start | bytes 6148
  253.0 12.6 copy-start.139
  254.4 30.8 %reduce-scatter.22.cloned.1.call-start = ((), (), s32[]{:S(2)}) async-start(), calls=%async_computation.22 | async-start | bytes 2359296 | tf_op jit(solution)/shard_map/reduce_scatter | solution.py:133
  274.9 25.5 %all-gather.19.cloned.1.call-start = ((), (), s32[]{:S(2)}) async-start(), calls=%async_computation.24 | async-start | bytes 2359296 | tf_op jit(solution)/shard_map/all_gather | solution.py:129
  289.2 35.2 %reduce-scatter.26.cloned.1.call-start = ((), (), s32[]{:S(2)}) async-start(), calls=%async_computation.25 | async-start | bytes 2359296 | tf_op jit(solution)/shard_map/reduce_scatter | solution.py:133
  314.1 29.3 %all-gather.21.cloned.1.call-start = ((), (), s32[]{:S(2)}) async-start(), calls=%async_computation.26 | async-start | bytes 2359296 | tf_op jit(solution)/shard_map/all_gather | solution.py:193
  332.2 36.7 %reduce-scatter.28.cloned.1.call-start = ((), (), s32[]{:S(2)}) async-start(), calls=%async_computation.27 | async-start | bytes 2359296 | tf_op jit(solution)/shard_map/reduce_scatter | solution.py:205
  358.5 29.6 %all-gather.23.cloned.1.call-start = ((), (), s32[]{:S(2)}) async-start(), calls=%async_computation.28 | async-start | bytes 2359296 | tf_op jit(solution)/shard_map/all_gather | solution.py:214
  358.6 14.5 %copy-start.115 = (f32[2,256]{1,0:T(2,128)}, f32[2,256]{1,0:T(2,128)S(1)}, u32[]{:S(2)}) copy-start(f32[2,256]{1,0:T(2,128)S(1)} %broadcast_multiply_fusion.4) | copy-start | bytes 6148
  377.0 63.3 %reduce-scatter.30.cloned.1.call-start = ((), (), s32[]{:S(2)}) async-start(), calls=%async_computation.29 | async-start | bytes 2359296 | tf_op jit(solution)/shard_map/reduce_scatter | solution.py:240
  429.9 28.7 %all-gather.27.cloned.1.call-start = ((), (), s32[]{:S(2)}) async-start(), calls=%async_computation.33 | async-start | bytes 2359296 | tf_op jit(solution)/shard_map/all_gather | solution.py:193
  443.6 24.8 %slice-start = ((s8[4718592]{0:T(1024)(128)(4,1)}), s8[524288]{0:T(1024)(128)(4,1)S(1)}, s32[]{:S(2)}) async-start(s8[4718592]{0:T(1024)(128)(4,1)} %bitcast.486), calls=%async_computation.41 | async-start | bytes 1048576
  445.7 12.9 copy-start.138
  447.4 35.2 %reduce-scatter.36.cloned.1.call-start = ((), (), s32[]{:S(2)}) async-start(), calls=%async_computation.34 | async-start | bytes 2359296 | tf_op jit(solution)/shard_map/reduce_scatter | solution.py:205
  468.4 14.2 %copy-start.87 = (f32[768]{0:T(1024)S(1)}, f32[768]{0:T(1024)}, u32[]{:S(2)}) copy-start(f32[768]{0:T(1024)} %copy-done.86) | copy-start | bytes 9220
  468.4 14.2 %copy-start.95 = (f32[768]{0:T(1024)S(1)}, f32[768]{0:T(1024)}, u32[]{:S(2)}) copy-start(f32[768]{0:T(1024)} %copy-done.94) | copy-start | bytes 9220
  468.4 14.2 %copy-start.111 = (f32[2,256]{1,0:T(2,128)S(1)}, f32[2,256]{1,0:T(2,128)}, u32[]{:S(2)}) copy-start(f32[2,256]{1,0:T(2,128)} %copy-done.110) | copy-start | bytes 6148
  472.2 13.2 %copy-start.118 = (f32[2,256]{1,0:T(2,128)S(1)}, f32[2,256]{1,0:T(2,128)}, u32[]{:S(2)}) copy-start(f32[2,256]{1,0:T(2,128)} %copy-done.117) | copy-start | bytes 6148
  472.2 27.7 %all-gather.29.cloned.1.call-start = ((), (), s32[]{:S(2)}) async-start(), calls=%async_computation.35 | async-start | bytes 2359296 | tf_op jit(solution)/shard_map/all_gather | solution.py:214
  487.6 12.3 copy-start.147
  488.7 200.5 %reduce-scatter.38.cloned.1.call-start = ((), (), s32[]{:S(2)}) async-start(), calls=%async_computation.36 | async-start | bytes 2359296 | tf_op jit(solution)/shard_map/reduce_scatter | solution.py:240
  543.5 253.3 %all-reduce.8.cloned.1.call-start = ((), (), s32[]{:S(2)}) async-start(), calls=%async_computation.40 | async-start | bytes 14155776
  566.2 362.7 %reduce-scatter.40.cloned.1.call-start = ((), (), s32[]{:S(2)}) async-start(), calls=%async_computation.37 | async-start | bytes 2506752 | tf_op jit(solution)/shard_map/reduce_scatter | solution.py:326
  572.5 533.6 %reduce-scatter.44.cloned.1.call-start = ((), (), s32[]{:S(2)}) async-start(), calls=%async_computation.39 | async-start | bytes 10027008 | tf_op jit(solution)/shard_map/reduce_scatter | solution.py:328
  586.2 695.7 %reduce-scatter.42.cloned.1.call-start = ((), (), s32[]{:S(2)}) async-start(), calls=%async_computation.38 | async-start | bytes 10027008 | tf_op jit(solution)/shard_map/reduce_scatter | solution.py:327
  605.0 84.1 %copy-start.26 = (f32[2,256,768]{2,1,0:T(8,128)S(1)}, f32[2,256,768]{2,1,0:T(8,128)}, u32[]{:S(2)}) copy-start(f32[2,256,768]{2,1,0:T(8,128)} %copy-done.25) | copy-start | bytes 4718596
  (159 other events, 425.3 us)
Sparse Core Ops, SparseCore 0:
  9.6 12.4 all-gather.10
  65.6 10.2 reduce-scatter.15
  83.3 10.2 reduce-scatter.31
  97.1 10.9 all-gather.12
  117.5 10.2 reduce-scatter.17
  132.6 10.9 all-gather.24
  157.4 10.2 reduce-scatter.33
  172.8 10.9 all-gather.14
  224.3 10.3 reduce-scatter.19
  240.7 10.2 reduce-scatter.23
  254.5 11.0 all-gather.16
  275.0 10.2 reduce-scatter.21
  289.4 10.9 all-gather.18
  314.2 10.2 reduce-scatter.25
  332.3 10.9 all-gather.20
  358.6 10.2 reduce-scatter.27
  377.1 10.9 all-gather.22
  430.0 10.2 reduce-scatter.29
  447.5 10.9 all-gather.26
  472.3 10.1 reduce-scatter.35
  488.8 11.0 all-gather.28
  543.6 10.2 reduce-scatter.37
  566.3 230.4 all-reduce.7
  802.1 126.6 reduce-scatter.39
  936.1 169.9 reduce-scatter.43
  1112.2 169.7 reduce-scatter.41
